TPU v7x, 32 devices: a whole 2x2x4 slice. The times are simulated.
32 devices in a mesh: grp: 4 (over z), mem: 8 (over y, x, core).
Axes of the slice: x: 2, y: 2, z: 4, core: 2. Of those that a mesh axis runs over, the one named last changes fastest.
Arguments:
- volume: float32 [4, 8, 8, 512, 1024], P('grp', 'mem'), may hold values from -1 to 1
- transfer_coef: float32 [4, 4], replicated, may hold values from -3 to 3
- group_order: int32 [4], replicated, may hold values from 0 to 3, each once
- member_order: int32 [4, 8], replicated, may hold values from 0 to 7, each once within a row
- active_mask: int32 [4, 8], P('grp', 'mem'), may hold values 0 or 1
Outputs:
- picture: float32 [4, 512, 1024], P(None, 'mem', 'grp')
All inputs are finite; a program needn't handle non-finite values. No bound on the sum of `active_mask` on one device may be relied on, other than what follows from the above.
Results may differ from a plain program's by a relative error of at most 0.0003.
Values sent between devices are 32-bit elements; how exact they have to be, the bound alone decides.
A program may use at most 192 MiB of HBM per device.

v0:
```python
import jax
import jax.numpy as jnp
from jax import lax
from jax.sharding import PartitionSpec as P


def polynomial(coef_row, values):
    return coef_row[0] + values * (coef_row[1] + values * (coef_row[2] + values * coef_row[3]))


def march_brick(samples, transfer_coef, active_flag, density_scale):
    optical_depth = jnp.zeros(samples.shape[1:], jnp.float32)
    colour = jnp.zeros((3,) + samples.shape[1:], jnp.float32)
    for sample_index in range(samples.shape[0]):
        values = samples[sample_index]
        extinction = polynomial(transfer_coef[3], values) ** 2 * density_scale
        opacity = 1.0 - jnp.exp(-extinction)
        tinted = jax.nn.sigmoid(
            jnp.stack([polynomial(transfer_coef[channel], values) for channel in range(3)])
        )
        colour = colour + (jnp.exp(-optical_depth) * opacity)[None] * tinted
        optical_depth = optical_depth + extinction
    coverage = 1.0 - jnp.exp(-optical_depth)
    return jnp.concatenate([colour, coverage[None]], 0) * active_flag


def reorder(layers, rank_list):
    total = rank_list.shape[0]
    positions = jnp.arange(total, dtype=jnp.int32)
    inverse = jnp.sum(
        positions[:, None] * (rank_list[:, None] == positions[None, :]).astype(jnp.int32), axis=0
    )
    return jnp.take(layers, inverse, axis=0)


def over_tree(layers):
    while layers.shape[0] > 1:
        nearer = layers[0::2]
        farther = layers[1::2]
        layers = nearer + (1.0 - nearer[:, 3:4]) * farther
    return layers[0]


def body(volume, transfer_coef, group_order, member_order, active_mask):
    groups = lax.axis_size("grp")
    members = lax.axis_size("mem")
    density_scale = 3.0 / (volume.shape[2] * groups * members)
    active_flag = active_mask[0, 0].astype(jnp.float32)
    layer = march_brick(volume[0, 0], transfer_coef, active_flag, density_scale)
    slab_ranks = lax.dynamic_slice_in_dim(member_order, lax.axis_index("grp"), 1, 0)[0]
    slab_image = over_tree(
        reorder(
            lax.all_to_all(layer[None], "mem", split_axis=2, concat_axis=0, tiled=True), slab_ranks
        )
    )
    return over_tree(
        reorder(
            lax.all_to_all(slab_image[None], "grp", split_axis=3, concat_axis=0, tiled=True),
            group_order,
        )
    )


def solution(mesh):
    in_specs = (P("grp", "mem", None, None, None), P(), P(), P(), P("grp", "mem"))
    out_specs = P(None, "mem", "grp")
    return jax.shard_map(body, mesh=mesh, in_specs=in_specs, out_specs=out_specs, check_vma=False)
```

profile of v0, /device:TPU:2, one launch (start us, length us, event | category | flops | bytes accessed | tf_op | source)
XLA Modules:
  0.0 448.7 jit_solution(17760567947958751179)
XLA Ops:
  0.0 0.0 copy-start
  0.0 0.0 copy-start.9
  0.0 6.7 %slice_bitcast_fusion = (f32[1,512,1024]{2,1,0:T(8,128)S(1)}, f32[1,1,1,512,1024]{4,3,2,1,0:T(8,128)S(1)}, f32[1,1,1,512,1024]{4,3,2,1,0:T(8,128)S(1)}, f32[1,1,...) fusion(f32[1,1,8,512,1024]{4,3,2,1,0:T(8,128)} %param.5), kind=kLoop, calls=%fused_computation.159 | loop fusion | bytes 33554432 | tf_op jit(solution)/shard_map/squeeze | solution.py:15
  6.7 0.0 copy-done.9
  6.7 0.0 copy-start.1
  6.7 0.9 fusion.105
  7.6 31.3 %multiply_add_fusion.4 = (f32[1,512,1024]{2,0,1:T(1,128)}, f32[1,512,1024]{2,0,1:T(1,128)}, f32[1,512,1024]{2,0,1:T(1,128)}, f32[1,512,1024]{2,0,1:T(1,128)}, f3...) fusion(f32[]{:T(128)} %bitcast.9, f32[]{:T(128)} %bitcast.8, f32[]{:T(128)} %bitcast.7, f32[]{:T(128)} %bitcast.6, ...), kind=kLoop, calls=%fused_computation.130 | loop fusion | flops 18874368 | bytes 16777264 | tf_op jit(solution)/shard_map/add | solution.py:8
  39.0 0.0 copy-done.1
  39.0 30.7 %multiply_add_fusion.10 = (f32[1,512,1024]{2,0,1:T(1,128)}, f32[1,512,1024]{2,0,1:T(1,128)}, f32[1,512,1024]{2,0,1:T(1,128)}, f32[1,512,1024]{2,0,1:T(1,128)}, f...) fusion(f32[1,1,1,512,1024]{4,3,2,1,0:T(8,128)S(1)} %get-tuple-element.16, f32[]{:T(128)} %bitcast.9, f32[]{:T(128)} %bitcast.8, ...), kind=kLoop, calls=%fused_computation.137 | loop fusion | flops 18874368 | bytes 16777264 | tf_op jit(solution)/shard_map/add | solution.py:8
  69.6 30.7 %multiply_add_fusion.16 = (f32[1,512,1024]{2,0,1:T(1,128)}, f32[1,512,1024]{2,0,1:T(1,128)}, f32[1,512,1024]{2,0,1:T(1,128)}, f32[1,512,1024]{2,0,1:T(1,128)}, f...) fusion(f32[1,1,1,512,1024]{4,3,2,1,0:T(8,128)S(1)} %get-tuple-element.18, f32[]{:T(128)} %bitcast.9, f32[]{:T(128)} %bitcast.8, ...), kind=kLoop, calls=%fused_computation.145 | loop fusion | flops 18874368 | bytes 16777264 | tf_op jit(solution)/shard_map/add | solution.py:8
  100.3 0.0 copy-start.2
  100.3 0.0 slice-start.1
  100.3 32.0 %multiply_add_fusion.22 = (f32[1,512,1024]{2,0,1:T(1,128)}, f32[1,512,1024]{2,0,1:T(1,128)}, f32[1,512,1024]{2,0,1:T(1,128)}, f32[1,512,1024]{2,0,1:T(1,128)}, f...) fusion(f32[1,1,1,512,1024]{4,3,2,1,0:T(8,128)S(1)} %get-tuple-element.20, f32[]{:T(128)} %bitcast.9, f32[]{:T(128)} %bitcast.8, ...), kind=kLoop, calls=%fused_computation.153 | loop fusion | flops 18874368 | bytes 16777264 | tf_op jit(solution)/shard_map/add | solution.py:8
  132.3 0.0 copy-done.2
  132.3 0.0 slice-start.2
  132.3 0.0 slice-start.3
  132.3 41.6 %fusion.86 = f32[1,1,512,1024]{3,1,0,2:T(1,128)} fusion(f32[1,1,1,512,1024]{4,3,2,1,0:T(8,128)S(1)} %get-tuple-element.16, f32[1,1,1,512,1024]{4,3,2,1,0:T(8,128)S(1)} %get-tuple-element.17, f32[1,1,1,512,1024]{4,3,2,1,0:T(8,128)S(1)} %get-tuple-element.18, f32[1,1,1,512,1024]{4,3,2,1,0:T(8,128)S(1)} %get-tuple-element.19, ...), kind=kLoop, calls=%fused_computation.126 | loop fusion | flops 34603008 | bytes 18874384 | tf_op jit(solution)/shard_map/concatenate | solution.py:24
  174.0 0.0 slice-done
  174.0 0.0 slice-done.1
  174.0 0.0 slice-done.2
  174.0 0.0 slice-done.3
  174.0 6.2 %subtract_multiply_fusion.3 = (f32[512,1024]{1,0:T(8,128)}, f32[512,1024]{1,0:T(8,128)S(1)}) fusion(f32[]{:T(128)} %bitcast.5, f32[]{:T(128)} %bitcast.4, f32[]{:T(128)} %bitcast.3, f32[]{:T(128)} %bitcast.1, f32[1,1,8,512,1024]{4,3,2,1,0:T(8,128)S(1)} %bitcast.282), kind=kLoop, calls=%fused_computation.146 | loop fusion | flops 19922944 | bytes 12582928 | tf_op jit(solution)/shard_map/mul | solution.py:21
  180.2 6.7 %subtract_multiply_fusion.1 = (f32[512,1024]{1,0:T(8,128)}, f32[512,1024]{1,0:T(8,128)S(1)}, f32[512,1024]{1,0:T(8,128)}) fusion(f32[]{:T(128)} %bitcast.5, f32[]{:T(128)} %bitcast.4, f32[]{:T(128)} %bitcast.3, f32[]{:T(128)} %bitcast.1, f32[1,1,8,512,1024]{4,3,2,1,0:T(8,128)S(1)} %bitcast.282, f32[512,1024]{1,0:T(8,128)S(1)} %get-tuple-element.6), kind=kLoop, calls=%fused_computation.138 | loop fusion | flops 17825792 | bytes 14680080 | tf_op jit(solution)/shard_map/mul | solution.py:21
  187.0 0.0 copy-start.3
  187.0 0.0 copy-start.4
  187.0 0.0 copy-start.7
  187.0 0.0 copy-start.8
  187.0 11.5 %subtract_multiply_fusion = (f32[512,1024]{1,0:T(8,128)}, f32[512,1024]{1,0:T(8,128)}, f32[512,1024]{1,0:T(8,128)}, f32[512,1024]{1,0:T(8,128)}, f32[512,1024]{1,0:T(8,128)}) fusion(f32[]{:T(128)} %bitcast.5, f32[]{:T(128)} %bitcast.4, f32[]{:T(128)} %bitcast.3, f32[]{:T(128)} %bitcast.1, f32[512,1024]{1,0:T(8,128)S(1)} %get-tuple-element.8, ...), kind=kLoop, calls=%fused_computation.134 | loop fusion | flops 35651584 | bytes 25165840 | tf_op jit(solution)/shard_map/mul | solution.py:21
  199.2 0.0 copy-done.3
  199.2 0.0 copy-done.4
  199.2 0.0 copy-done.5
  199.2 0.0 copy-done.6
  199.2 0.0 copy-done.7
  199.2 0.0 copy-done.8
  199.2 75.1 %fusion.39 = f32[1,3,512,1024]{3,1,0,2:T(4,128)S(1)} fusion(f32[1,512,1024]{2,0,1:T(1,128)S(1)} %copy-done.4, f32[1,512,1024]{2,0,1:T(1,128)S(1)} %copy-done.5, f32[1,512,1024]{2,0,1:T(1,128)S(1)} %copy-done.3, f32[1,512,1024]{2,0,1:T(1,128)S(1)} %copy-done.6, f32[1,512,1024]{2,0,1:T(1,128)S(1)} %copy-done.7, f32[1,512,1024]{2,0,1:T(1,128)S(1)} %copy-done.8, ...), kind=kLoop, calls=%fused_computation.51 | loop fusion | flops 86507520 | bytes 73400320 | tf_op jit(solution)/shard_map/concatenate | solution.py:24
  274.3 7.1 %maximum_multiply_fusion = f32[1,4,512,1024]{3,1,0,2:T(4,128)} fusion(f32[1,1,512,1024]{3,1,0,2:T(1,128)} %fusion.86, f32[1,3,512,1024]{3,1,0,2:T(4,128)S(1)} %fusion.39, f32[]{:T(128)} %bitcast.29), kind=kLoop, calls=%fused_computation.49 | loop fusion | flops 4194304 | bytes 16777220 | tf_op jit(solution)/shard_map/mul | solution.py:24
  281.4 5.1 %all-to-all-start = ((f32[1,4,512,1024]{3,1,0,2:T(4,128)}), f32[1,4,512,1024]{3,1,0,2:T(4,128)}, u32[]{:S(2)}, u32[]{:S(2)}) async-start(f32[1,4,512,1024]{3,1,0,2:T(4,128)} %maximum_multiply_fusion), calls=%async_computation | async-start | bytes 16777216 | tf_op jit(solution)/shard_map/all_to_all | solution.py:53
  286.5 0.0 copy-done
  286.5 0.1 select_reduce_fusion
  286.6 92.2 %all-to-all-done = f32[1,4,512,1024]{3,1,0,2:T(4,128)} async-done(((f32[1,4,512,1024]{3,1,0,2:T(4,128)}), f32[1,4,512,1024]{3,1,0,2:T(4,128)}, u32[]{:S(2)}, u32[]{:S(2)}) %all-to-all-start) | async-done | bytes 8388640 | tf_op jit(solution)/shard_map/all_to_all | solution.py:53
  378.8 11.3 %copy.99 = f32[1,4,8,64,1024]{4,3,1,2,0:T(8,128)} copy(f32[1,4,8,64,1024]{4,1,3,2,0:T(4,128)} %bitcast.30) | data formatting | bytes 16777216 | tf_op jit(solution)/shard_map/all_to_all | solution.py:53
  390.1 7.7 %gather_fusion = f32[8,4,64,1024]{3,2,1,0:T(8,128)} fusion(f32[8,4,64,1024]{3,2,1,0:T(8,128)} %bitcast.283, s32[1024]{0:T(1024)S(1)} %pad_clamp_fusion.1), kind=kCustom, calls=%fused_computation | custom fusion | bytes 16777248 | tf_op jit(solution)/shard_map/jit(_take)/gather | solution.py:33
  397.9 4.4 broadcast_select_fusion
  402.3 0.5 slice.148
  402.8 0.1 fusion.94
  402.9 1.1 multiply_add_fusion
  404.1 0.1 slice.151
  404.3 0.7 multiply_add_fusion.1
  405.0 0.2 fusion.93
  405.2 0.9 copy.75
  406.1 0.0 copy-start.10
  406.1 2.9 reshape.2041
  409.0 5.4 %all-to-all-start.1 = ((f32[4,1,65536]{2,1,0:T(1,128)}), f32[4,1,65536]{2,1,0:T(1,128)S(1)}, u32[]{:S(2)}, u32[]{:S(2)}) async-start(f32[4,1,65536]{2,1,0:T(1,128)} %reshape.2041), calls=%async_computation.1 | async-start | bytes 2097152 | tf_op jit(solution)/shard_map/all_to_all | solution.py:58
  414.5 0.0 copy-done.10
  414.5 0.1 select_reduce_fusion.1
  414.6 25.8 %all-to-all-done.1 = f32[4,1,65536]{2,1,0:T(1,128)S(1)} async-done(((f32[4,1,65536]{2,1,0:T(1,128)}), f32[4,1,65536]{2,1,0:T(1,128)S(1)}, u32[]{:S(2)}, u32[]{:S(2)}) %all-to-all-start.1) | async-done | bytes 1048608 | tf_op jit(solution)/shard_map/all_to_all | solution.py:58
  440.4 0.5 broadcast.2075
  441.0 3.8 reduce
  444.7 1.4 reshape.2042
  446.2 0.8 copy.77
  447.0 0.6 gather_fusion.1
  447.6 0.2 broadcast_select_fusion.1
  447.9 0.1 multiply_add_fusion.26
  448.0 0.7 fusion.97
  (16 shorter events, 0.2 us)
Async XLA Ops:
  0.0 286.5 %copy-start = (s32[4,8]{1,0:T(4,128)S(1)}, s32[4,8]{1,0:T(4,128)}, u32[]{:S(2)}) copy-start(s32[4,8]{1,0:T(4,128)} %param.8) | copy-start | bytes 388
  0.0 6.7 %copy-start.9 = (f32[4,4]{1,0:T(4,128)S(1)}, f32[4,4]{1,0:T(4,128)}, u32[]{:S(2)}) copy-start(f32[4,4]{1,0:T(4,128)} %param.6) | copy-start | bytes 196
  6.7 32.2 %copy-start.1 = (f32[1,1,1,512,1024]{4,3,2,1,0:T(8,128)}, f32[1,1,1,512,1024]{4,3,2,1,0:T(8,128)S(1)}, u32[]{:S(2)}) copy-start(f32[1,1,1,512,1024]{4,3,2,1,0:T(8,128)S(1)} %get-tuple-element.22) | copy-start | bytes 6291460
  100.3 32.0 %copy-start.2 = (f32[1,1,1,512,1024]{4,3,2,1,0:T(8,128)S(1)}, f32[1,1,1,512,1024]{4,3,2,1,0:T(8,128)}, u32[]{:S(2)}) copy-start(f32[1,1,1,512,1024]{4,3,2,1,0:T(8,128)} %copy-done.1) | copy-start | bytes 6291460
  100.3 73.6 %slice-start = ((s8[16777216]{0:T(1024)(128)(4,1)}), s8[4194304]{0:T(1024)(128)(4,1)S(1)}, s32[]{:S(2)}) async-start(s8[16777216]{0:T(1024)(128)(4,1)} %bitcast.281), calls=%async_computation.2 | async-start | bytes 8388608
  100.3 73.6 %slice-start.1 = ((s8[16777216]{0:T(1024)(128)(4,1)}), s8[4194304]{0:T(1024)(128)(4,1)S(1)}, s32[]{:S(2)}) async-start(s8[16777216]{0:T(1024)(128)(4,1)} %bitcast.281), calls=%async_computation.3 | async-start | bytes 8388608
  132.3 41.6 %slice-start.2 = ((s8[16777216]{0:T(1024)(128)(4,1)}), s8[4194304]{0:T(1024)(128)(4,1)S(1)}, s32[]{:S(2)}) async-start(s8[16777216]{0:T(1024)(128)(4,1)} %bitcast.281), calls=%async_computation.4 | async-start | bytes 8388608
  132.3 41.6 %slice-start.3 = ((s8[16777216]{0:T(1024)(128)(4,1)}), s8[4194304]{0:T(1024)(128)(4,1)S(1)}, s32[]{:S(2)}) async-start(s8[16777216]{0:T(1024)(128)(4,1)} %bitcast.281), calls=%async_computation.5 | async-start | bytes 8388608
  187.0 12.2 %copy-start.3 = (f32[1,512,1024]{2,0,1:T(1,128)S(1)}, f32[1,512,1024]{2,0,1:T(1,128)}, u32[]{:S(2)}) copy-start(f32[1,512,1024]{2,0,1:T(1,128)} %get-tuple-element.44) | copy-start | bytes 6291460
  187.0 12.2 %copy-start.4 = (f32[1,512,1024]{2,0,1:T(1,128)S(1)}, f32[1,512,1024]{2,0,1:T(1,128)}, u32[]{:S(2)}) copy-start(f32[1,512,1024]{2,0,1:T(1,128)} %get-tuple-element.45) | copy-start | bytes 6291460
  187.0 12.2 %copy-start.5 = (f32[1,512,1024]{2,0,1:T(1,128)S(1)}, f32[1,512,1024]{2,0,1:T(1,128)}, u32[]{:S(2)}) copy-start(f32[1,512,1024]{2,0,1:T(1,128)} %get-tuple-element.46) | copy-start | bytes 6291460
  187.0 12.2 %copy-start.6 = (f32[1,512,1024]{2,0,1:T(1,128)S(1)}, f32[1,512,1024]{2,0,1:T(1,128)}, u32[]{:S(2)}) copy-start(f32[1,512,1024]{2,0,1:T(1,128)} %get-tuple-element.63) | copy-start | bytes 6291460
  187.0 12.2 %copy-start.7 = (f32[1,512,1024]{2,0,1:T(1,128)S(1)}, f32[1,512,1024]{2,0,1:T(1,128)}, u32[]{:S(2)}) copy-start(f32[1,512,1024]{2,0,1:T(1,128)} %get-tuple-element.64) | copy-start | bytes 6291460
  187.0 12.2 %copy-start.8 = (f32[1,512,1024]{2,0,1:T(1,128)S(1)}, f32[1,512,1024]{2,0,1:T(1,128)}, u32[]{:S(2)}) copy-start(f32[1,512,1024]{2,0,1:T(1,128)} %get-tuple-element.65) | copy-start | bytes 6291460
  281.4 97.5 %all-to-all-start = ((f32[1,4,512,1024]{3,1,0,2:T(4,128)}), f32[1,4,512,1024]{3,1,0,2:T(4,128)}, u32[]{:S(2)}, u32[]{:S(2)}) async-start(f32[1,4,512,1024]{3,1,0,2:T(4,128)} %maximum_multiply_fusion), calls=%async_computation | async-start | bytes 16777216 | tf_op jit(solution)/shard_map/all_to_all | solution.py:53
  406.1 8.4 %copy-start.10 = (s32[4]{0:T(128)S(1)}, s32[4]{0:T(128)}, u32[]{:S(2)}) copy-start(s32[4]{0:T(128)} %param.7) | copy-start | bytes 52
  409.0 31.4 %all-to-all-start.1 = ((f32[4,1,65536]{2,1,0:T(1,128)}), f32[4,1,65536]{2,1,0:T(1,128)S(1)}, u32[]{:S(2)}, u32[]{:S(2)}) async-start(f32[4,1,65536]{2,1,0:T(1,128)} %reshape.2041), calls=%async_computation.1 | async-start | bytes 2097152 | tf_op jit(solution)/shard_map/all_to_all | solution.py:58
where the time goes:
time: 450 us; the launch traced here: 449 us
  other arithmetic  285 us (63%)
  waiting for transfers between devices  118 us (26%)
  local copies, waits for them, and re-layouts  34.6 us (8%)
  starting transfers between devices  10.6 us (2%)
    add x4, other arithmetic, polynomial(): coef_row[0]  125 us
    concatenate x2, other arithmetic, march_brick(): return jnp.concatenate([colour, coverage[None]], 0) * active_flag  117 us
    all_to_all x1, waiting for transfers between devices, body(): lax.all_to_all(layer[None], 'mem', split_axis=2, concat_axis=0, tiled=True)  92.2 us
    all_to_all x1, waiting for transfers between devices, body(): lax.all_to_all(slab_image[None], 'grp', split_axis=3, concat_axis=0, tile...  25.8 us
    mul x3, other arithmetic, march_brick(): colour = colour + (jnp.exp(-optical_depth) * opacity)[None] * tinted  24.5 us
    all_to_all x1, local copies, waits for them, and re-layouts, body(): lax.all_to_all(layer[None], 'mem', split_axis=2, concat_axis=0, tiled=True)  11.3 us
  transfers between devices with their start and end apart: 2, of which 2 were waited for; matrix products, arithmetic and copies ran while one was open for 0% of the time, Pallas kernels for 0%

commit v1 on v0

--- a/solution.py
+++ b/solution.py
@@ -42,17 +42,31 @@
 
 
 def body(volume, transfer_coef, group_order, member_order, active_mask):
+
+    def field_cut(q_in):
+        val, t1 = (lax.axis_size("mem"), lax.axis_index("mem"))
+        base_arr = q_in.shape[2] // val
+        s_next = list(q_in.shape)
+        s_next[2] = base_arr
+        kept_arr = s_next[0]
+        s_next[0] = kept_arr * val
+        block_last = jnp.zeros(s_next, q_in.dtype)
+        for ix in range(val):
+            moved = lax.dynamic_slice_in_dim(q_in, (t1 ^ ix) * base_arr, base_arr, axis=2)
+            if ix:
+                moved = lax.ppermute(moved, "mem", perm=[(m, m ^ ix) for m in range(val)])
+            block_last = lax.dynamic_update_slice_in_dim(
+                block_last, moved, (t1 ^ ix) * kept_arr, axis=0
+            )
+        return block_last
+
     groups = lax.axis_size("grp")
     members = lax.axis_size("mem")
     density_scale = 3.0 / (volume.shape[2] * groups * members)
     active_flag = active_mask[0, 0].astype(jnp.float32)
     layer = march_brick(volume[0, 0], transfer_coef, active_flag, density_scale)
     slab_ranks = lax.dynamic_slice_in_dim(member_order, lax.axis_index("grp"), 1, 0)[0]
-    slab_image = over_tree(
-        reorder(
-            lax.all_to_all(layer[None], "mem", split_axis=2, concat_axis=0, tiled=True), slab_ranks
-        )
-    )
+    slab_image = over_tree(reorder(field_cut(layer[None]), slab_ranks))
     return over_tree(
         reorder(
             lax.all_to_all(slab_image[None], "grp", split_axis=3, concat_axis=0, tiled=True),

time: 450 us -> 281 us (0.62)
  other arithmetic: 285 us -> 126 us
  waiting for transfers between devices: 118 us -> 99 us
  local copies, waits for them, and re-layouts: 34.6 us -> 42.7 us
    concatenate x2 -> x0, other arithmetic: 117 us -> none  [march_brick(): return jnp.concatenate([colour, coverage[None]], 0) * active_flag]
    all_to_all x1 -> x0, waiting for transfers between devices: 92.2 us -> none  [body(): lax.all_to_all(layer[None], 'mem', split_axis=2, concat_axis=0, tiled=True)]
    ppermute x0 -> x7, waiting for transfers between devices: none -> 72.4 us  [field_cut(): moved = lax.ppermute(moved, 'mem', perm=[(m, m ^ ix) for m in range(val)])]
    add x4, other arithmetic: 125 us -> 53.3 us  [polynomial(): coef_row[0]]
    add x0 -> x1, other arithmetic: none -> 23.5 us  [march_brick(): colour = colour + (jnp.exp(-optical_depth) * opacity)[None] * tinted]
    dynamic_update_slice x0 -> x8, local copies, waits for them, and re-layouts: none -> 16.2 us  [field_cut(): lax.dynamic_update_slice_in_dim(block_last, moved, (t1 ^ ix) * kept_arr,...]
    sub x0 -> x2, other arithmetic: none -> 15.8 us  [the longest x1 8.02 us: march_brick(): opacity = 1.0 - jnp.exp(-extinction)]
    all_to_all x1 -> x0, local copies, waits for them, and re-layouts: 11.3 us -> none  [body(): lax.all_to_all(layer[None], 'mem', split_axis=2, concat_axis=0, tiled=True)]
  transfers between devices with their start and end apart: 2 -> 8, of which waited for: 2 -> 4; matrix products, arithmetic and copies ran while one was open for 0% -> 7% of each run, Pallas kernels for 0% -> 0%
where the time goes in v1:
time: 281 us; the launch traced here: 279 us
  other arithmetic  126 us (45%)
  waiting for transfers between devices  99 us (35%)
  local copies, waits for them, and re-layouts  42.7 us (15%)
  starting transfers between devices  10.2 us (4%)
    ppermute x7, waiting for transfers between devices, field_cut(): moved = lax.ppermute(moved, 'mem', perm=[(m, m ^ ix) for m in range(val)])  72.4 us
    add x4, other arithmetic, polynomial(): coef_row[0]  53.3 us
    all_to_all x1, waiting for transfers between devices, body(): lax.all_to_all(slab_image[None], 'grp', split_axis=3, concat_axis=0, tile...  26.7 us
    add x1, other arithmetic, march_brick(): colour = colour + (jnp.exp(-optical_depth) * opacity)[None] * tinted  23.5 us
    mul x2, other arithmetic, march_brick(): colour = colour + (jnp.exp(-optical_depth) * opacity)[None] * tinted  17.1 us
    dynamic_update_slice x8, local copies, waits for them, and re-layouts, field_cut(): lax.dynamic_update_slice_in_dim(block_last, moved, (t1 ^ ix) * kept_arr,...  16.2 us
    gather x2, local copies, waits for them, and re-layouts, reorder(): return jnp.take(layers, inverse, axis=0)  8.31 us
    sub x1, other arithmetic, march_brick(): opacity = 1.0 - jnp.exp(-extinction)  8.02 us
  transfers between devices with their start and end apart: 8, of which 4 were waited for; matrix products, arithmetic and copies ran while one was open for 7% of the time, Pallas kernels for 0%

profile of v1, /device:TPU:2, one launch (start us, length us, event | category | flops | bytes accessed | tf_op | source)
XLA Modules:
  0.0 278.7 jit_solution(6859009751352361616)
XLA Ops:
  0.0 0.0 copy-start
  0.0 2.0 fusion.217
  2.0 0.0 copy-start.1
  2.0 16.1 %fusion.41 = (f32[1,512,1024]{2,1,0:T(8,128)S(1)}, f32[1,512,1024]{2,1,0:T(8,128)}, f32[1,512,1024]{2,1,0:T(8,128)}, f32[1,512,1024]{2,1,0:T(8,128)}, f32[1,512,...) fusion(f32[1,1,8,512,1024]{4,3,2,1,0:T(8,128)} %param.5, f32[]{:T(128)} %bitcast.10, f32[]{:T(128)} %bitcast.9, ...), kind=kLoop, calls=%fused_computation.66 | loop fusion | flops 22020096 | bytes 20971568 | tf_op jit(solution)/shard_map/add | solution.py:8
  18.1 0.0 copy-done.1
  18.1 13.2 %fusion.44 = (f32[1,512,1024]{2,1,0:T(8,128)}, f32[1,512,1024]{2,1,0:T(8,128)}, f32[1,512,1024]{2,1,0:T(8,128)}, f32[1,512,1024]{2,1,0:T(8,128)}, f32[1,512,1024...) fusion(f32[1,1,8,512,1024]{4,3,2,1,0:T(8,128)S(1)} %copy-done.1, f32[]{:T(128)} %bitcast.14, ...), kind=kLoop, calls=%fused_computation.69 | loop fusion | flops 22020096 | bytes 20971568 | tf_op jit(solution)/shard_map/add | solution.py:8
  31.3 13.2 %fusion.47 = (f32[1,512,1024]{2,1,0:T(8,128)}, f32[1,512,1024]{2,1,0:T(8,128)}, f32[1,512,1024]{2,1,0:T(8,128)}, f32[1,512,1024]{2,1,0:T(8,128)}, f32[1,512,1024...) fusion(f32[1,1,8,512,1024]{4,3,2,1,0:T(8,128)S(1)} %copy-done.1, f32[]{:T(128)} %bitcast.18, ...), kind=kLoop, calls=%fused_computation.72 | loop fusion | flops 22020096 | bytes 20971568 | tf_op jit(solution)/shard_map/add | solution.py:8
  44.5 10.8 %fusion.68 = (f32[1,512,1024]{2,1,0:T(8,128)}, f32[1,512,1024]{2,1,0:T(8,128)}, f32[1,512,1024]{2,1,0:T(8,128)}) fusion(f32[1,1,8,512,1024]{4,3,2,1,0:T(8,128)S(1)} %copy-done.1, f32[]{:T(128)} %bitcast.10, f32[]{:T(128)} %bitcast.9, f32[]{:T(128)} %bitcast.8, f32[]{:T(128)} %bitcast.6, f32[]{:T(128)} %bitcast.18, f32[]{:T(128)} %bitcast.17, f32[]{:T(128)} %bitcast.16, ...), kind=kLoop, calls=%fused_computation.108 | loop fusion | flops 9437184 | bytes 8388656 | tf_op jit(solution)/shard_map/add | solution.py:8
  55.3 8.0 %fusion.198 = (f32[512,1024]{1,0:T(8,128)}, f32[512,1024]{1,0:T(8,128)}, f32[512,1024]{1,0:T(8,128)}, f32[512,1024]{1,0:T(8,128)}, f32[512,1024]{1,0:T(8,128)}) fusion(f32[]{:T(128)} %bitcast.5, f32[]{:T(128)} %bitcast.4, f32[]{:T(128)} %bitcast.3, f32[1,1,8,512,1024]{4,3,2,1,0:T(8,128)S(1)} %copy-done.1, f32[]{:T(128)} %bitcast.1), kind=kLoop, calls=%fused_computation.339 | loop fusion | flops 24641536 | bytes 18874384 | tf_op jit(solution)/shard_map/sub | solution.py:17
  63.3 7.8 %fusion.56 = f32[1,512,1024]{2,1,0:T(8,128)} fusion(f32[1,1,8,512,1024]{4,3,2,1,0:T(8,128)S(1)} %copy-done.1, f32[]{:T(128)} %bitcast.5, f32[]{:T(128)} %bitcast.4, f32[]{:T(128)} %bitcast.3, f32[]{:T(128)} %bitcast.1), kind=kLoop, calls=%fused_computation.81 | loop fusion | flops 34603008 | bytes 18874384 | tf_op jit(solution)/shard_map/sub | solution.py:23
  71.1 8.6 %subtract_multiply_fusion.1 = (f32[512,1024]{1,0:T(8,128)}, f32[512,1024]{1,0:T(8,128)S(1)}, f32[512,1024]{1,0:T(8,128)}) fusion(f32[]{:T(128)} %bitcast.5, f32[]{:T(128)} %bitcast.4, f32[]{:T(128)} %bitcast.3, f32[1,1,8,512,1024]{4,3,2,1,0:T(8,128)} %param.5, f32[]{:T(128)} %bitcast.1, f32[512,1024]{1,0:T(8,128)} %get-tuple-element.16), kind=kLoop, calls=%fused_computation.333 | loop fusion | flops 17825792 | bytes 14680080 | tf_op jit(solution)/shard_map/mul | solution.py:21
  79.7 8.5 %subtract_multiply_fusion = (f32[512,1024]{1,0:T(8,128)}, f32[512,1024]{1,0:T(8,128)}) fusion(f32[]{:T(128)} %bitcast.5, f32[]{:T(128)} %bitcast.4, f32[]{:T(128)} %bitcast.3, f32[1,1,8,512,1024]{4,3,2,1,0:T(8,128)} %param.5, f32[]{:T(128)} %bitcast.1, f32[512,1024]{1,0:T(8,128)S(1)} %get-tuple-element.8), kind=kLoop, calls=%fused_computation.332 | loop fusion | flops 17825792 | bytes 12582928 | tf_op jit(solution)/shard_map/mul | solution.py:21
  88.9 23.5 %fusion.10 = f32[3,512,1024]{2,1,0:T(8,128)} fusion(f32[1,512,1024]{2,1,0:T(8,128)} %get-tuple-element.19, f32[1,512,1024]{2,1,0:T(8,128)} %get-tuple-element.20, f32[1,512,1024]{2,1,0:T(8,128)} %get-tuple-element.18, f32[1,512,1024]{2,1,0:T(8,128)} %get-tuple-element.22, f32[1,512,1024]{2,1,0:T(8,128)} %get-tuple-element.23, ...), kind=kLoop, calls=%fused_computation.14 | loop fusion | flops 86507520 | bytes 73400320 | tf_op jit(solution)/shard_map/add | solution.py:21
  112.4 4.4 %maximum_multiply_fusion = f32[4,512,1024]{2,1,0:T(8,128)S(1)} fusion(f32[1,512,1024]{2,1,0:T(8,128)} %fusion.56, f32[3,512,1024]{2,1,0:T(8,128)} %fusion.10, f32[]{:T(128)} %bitcast.33), kind=kLoop, calls=%fused_computation.2 | loop fusion | flops 4194304 | bytes 16777220 | tf_op jit(solution)/shard_map/mul | solution.py:24
  116.9 0.0 copy-start.2
  116.9 2.9 %dynamic-slice_bitcast_fusion = (f32[1,4,64,1024]{3,2,1,0:T(8,128)S(1)}, f32[1,4,64,1024]{3,2,1,0:T(8,128)S(1)}, f32[1,4,64,1024]{3,2,1,0:T(8,128)S(1)}, f32[1,4...) fusion(f32[4,512,1024]{2,1,0:T(8,128)S(1)} %maximum_multiply_fusi, ...), kind=kLoop, calls=%fused_computation.345 | loop fusion | bytes 14680092 | tf_op jit(solution)/shard_map/dynamic_slice | solution.py:55
  119.8 1.7 copy-done.2
  121.4 0.0 collective-permute-start
  121.4 0.0 collective-permute-start.1
  121.4 1.9 collective-permute-start.2
  123.3 1.5 collective-permute-start.3
  124.8 0.1 collective-permute-start.4
  124.9 0.1 select_reduce_fusion
  125.1 0.0 collective-permute-done
  125.1 1.6 collective-permute-start.5
  126.7 4.3 %broadcast_in_dim.21 = f32[8,4,64,1024]{3,2,1,0:T(8,128)} broadcast(f32[]{:T(128)} %constant.23.clone.1), dimensions={} | broadcast | bytes 8388612 | tf_op jit(solution)/shard_map/broadcast_in_dim | solution.py:53
  131.0 2.3 bitcast_dynamic-update-slice_fusion
  133.3 14.5 %collective-permute-done.1 = f32[1,4,64,1024]{3,2,1,0:T(8,128)} collective-permute-done((f32[1,4,64,1024]{3,2,1,0:T(8,128)}, f32[1,4,64,1024]{3,2,1,0:T(8,128)}, u32[]{:S(2)}, u32[]{:S(2)}) %collective-permute-start.1) | collective-permute-done | bytes 1048608 | tf_op jit(solution)/shard_map/ppermute | solution.py:57
  147.8 0.3 collective-permute-start.6
  148.1 2.3 constant_dynamic-update-slice_fusion.6
  150.4 2.4 constant_dynamic-update-slice_fusion.5
  152.8 16.5 %collective-permute-done.2 = f32[1,4,64,1024]{3,2,1,0:T(8,128)} collective-permute-done((f32[1,4,64,1024]{3,2,1,0:T(8,128)}, f32[1,4,64,1024]{3,2,1,0:T(8,128)}, u32[]{:S(2)}, u32[]{:S(2)}) %collective-permute-start.2) | collective-permute-done | bytes 1048608 | tf_op jit(solution)/shard_map/ppermute | solution.py:57
  169.3 2.3 constant_dynamic-update-slice_fusion.4
  171.6 0.0 collective-permute-done.3
  171.6 2.3 constant_dynamic-update-slice_fusion.3
  173.9 41.4 %collective-permute-done.4 = f32[1,4,64,1024]{3,2,1,0:T(8,128)} collective-permute-done((f32[1,4,64,1024]{3,2,1,0:T(8,128)S(1)}, f32[1,4,64,1024]{3,2,1,0:T(8,128)}, u32[]{:S(2)}, u32[]{:S(2)}) %collective-permute-start.4) | collective-permute-done | bytes 1048608 | tf_op jit(solution)/shard_map/ppermute | solution.py:57
  215.3 2.3 constant_dynamic-update-slice_fusion.2
  217.6 0.0 collective-permute-done.5
  217.6 1.1 constant_dynamic-update-slice_fusion.1
  218.7 0.0 collective-permute-done.6
  218.7 1.1 constant_dynamic-update-slice_fusion
  219.8 7.7 %gather_fusion = f32[8,4,64,1024]{3,2,1,0:T(8,128)} fusion(f32[8,4,64,1024]{3,2,1,0:T(8,128)} %constant_dynamic-update-slice_fusion, s32[1024]{0:T(1024)S(1)} %pad_clamp_fusion.1), kind=kCustom, calls=%fused_computation | custom fusion | bytes 16777248 | tf_op jit(solution)/shard_map/jit(_take)/gather | solution.py:33
  227.5 4.4 %broadcast_select_fusion = f32[8,4,64,1024]{3,2,1,0:T(8,128)S(1)} fusion(f32[8,4,64,1024]{3,2,1,0:T(8,128)} %gather_fusion, pred[8]{0:T(512)(128)(4,1)S(1)} %compare_and_fusion), kind=kLoop, calls=%fused_computation.51 | loop fusion | flops 2097152 | bytes 16777224 | tf_op jit(solution)/shard_map/jit(_take)/select_n | solution.py:33
  232.0 0.5 slice.148
  232.5 0.1 fusion.200
  232.6 1.1 multiply_add_fusion
  233.7 0.1 slice.151
  233.9 0.7 multiply_add_fusion.1
  234.7 0.2 fusion.199
  234.9 0.9 copy.12
  235.8 0.0 copy-start.3
  235.8 2.9 %reshape.1672 = f32[4,1,65536]{2,1,0:T(1,128)} reshape(f32[1024,1,4,64]{3,2,1,0:T(4,128)S(1)} %bitcast.740) | data formatting | bytes 2097152
  238.7 4.9 %all-to-all-start = ((f32[4,1,65536]{2,1,0:T(1,128)}), f32[4,1,65536]{2,1,0:T(1,128)S(1)}, u32[]{:S(2)}, u32[]{:S(2)}) async-start(f32[4,1,65536]{2,1,0:T(1,128)} %reshape.1672), calls=%async_computation | async-start | bytes 2097152 | tf_op jit(solution)/shard_map/all_to_all | solution.py:72
  243.6 0.0 copy-done.3
  243.6 0.1 select_reduce_fusion.1
  243.7 26.7 %all-to-all-done = f32[4,1,65536]{2,1,0:T(1,128)S(1)} async-done(((f32[4,1,65536]{2,1,0:T(1,128)}), f32[4,1,65536]{2,1,0:T(1,128)S(1)}, u32[]{:S(2)}, u32[]{:S(2)}) %all-to-all-start) | async-done | bytes 1048608 | tf_op jit(solution)/shard_map/all_to_all | solution.py:72
  270.4 0.5 broadcast.1697
  270.9 3.8 %reduce = f32[4,65536]{1,0:T(4,128)S(1)} reduce(f32[4,1,65536]{2,1,0:T(1,128)S(1)} %all-to-all-done, f32[]{:T(128)} %broadcast.1697), dimensions={1}, to_apply=%all_to_all.13.reduce_sub_computation | reduce | bytes 2097156 | tf_op jit(solution)/shard_map/all_to_all | solution.py:72
  274.7 1.4 reshape.1673
  276.1 0.8 copy.14
  276.9 0.6 gather_fusion.1
  277.6 0.2 broadcast_select_fusion.1
  277.8 0.1 multiply_add_fusion.2
  277.9 0.7 fusion.208
  (13 shorter events, 0.2 us)
Async XLA Ops:
  0.0 124.9 %copy-start = (s32[4,8]{1,0:T(4,128)S(1)}, s32[4,8]{1,0:T(4,128)}, u32[]{:S(2)}) copy-start(s32[4,8]{1,0:T(4,128)} %param.8) | copy-start | bytes 388
  2.0 16.1 %copy-start.1 = (f32[1,1,8,512,1024]{4,3,2,1,0:T(8,128)S(1)}, f32[1,1,8,512,1024]{4,3,2,1,0:T(8,128)}, u32[]{:S(2)}) copy-start(f32[1,1,8,512,1024]{4,3,2,1,0:T(8,128)} %param.5) | copy-start | bytes 50331652
  116.9 4.6 %copy-start.2 = (f32[4,512,1024]{2,1,0:T(8,128)}, f32[4,512,1024]{2,1,0:T(8,128)S(1)}, u32[]{:S(2)}) copy-start(f32[4,512,1024]{2,1,0:T(8,128)S(1)} %maximum_multiply_fusion) | copy-start | bytes 25165828
  121.4 3.7 %collective-permute-start = (f32[1,4,64,1024]{3,2,1,0:T(8,128)}, f32[1,4,64,1024]{3,2,1,0:T(8,128)}, u32[]{:S(2)}, u32[]{:S(2)}) collective-permute-start(f32[1,4,64,1024]{3,2,1,0:T(8,128)} %get-tuple-element.47), channel_id=1, source_target_pairs={{0,1},{1,0},{2,3},{3,2},{4,5},{5,4},{6,7},{7,6},{8,9},{9,8},{10,11... | collective-permute-start | bytes 3145736 | tf_op jit(solution)/shard_map/ppermute | solution.py:57
  121.4 26.3 %collective-permute-start.1 = (f32[1,4,64,1024]{3,2,1,0:T(8,128)}, f32[1,4,64,1024]{3,2,1,0:T(8,128)}, u32[]{:S(2)}, u32[]{:S(2)}) collective-permute-start(f32[1,4,64,1024]{3,2,1,0:T(8,128)} %get-tuple-element.46), channel_id=1, source_target_pairs={{0,2},{1,3},{2,0},{3,1},{4,6},{5,7},{6,4},{7,5},{8,10},{9,11},{10,... | collective-permute-start | bytes 3145736 | tf_op jit(solution)/shard_map/ppermute | solution.py:57
  121.4 47.9 %collective-permute-start.2 = (f32[1,4,64,1024]{3,2,1,0:T(8,128)}, f32[1,4,64,1024]{3,2,1,0:T(8,128)}, u32[]{:S(2)}, u32[]{:S(2)}) collective-permute-start(f32[1,4,64,1024]{3,2,1,0:T(8,128)} %get-tuple-element.45), channel_id=1, source_target_pairs={{0,3},{1,2},{2,1},{3,0},{4,7},{5,6},{6,5},{7,4},{8,11},{9,10},{10,... | collective-permute-start | bytes 3145736 | tf_op jit(solution)/shard_map/ppermute | solution.py:57
  123.3 48.3 %collective-permute-start.3 = (f32[1,4,64,1024]{3,2,1,0:T(8,128)}, f32[1,4,64,1024]{3,2,1,0:T(8,128)}, u32[]{:S(2)}, u32[]{:S(2)}) collective-permute-start(f32[1,4,64,1024]{3,2,1,0:T(8,128)} %get-tuple-element.44), channel_id=1, source_target_pairs={{0,4},{1,5},{2,6},{3,7},{4,0},{5,1},{6,2},{7,3},{8,12},{9,13},{10,... | collective-permute-start | bytes 3145736 | tf_op jit(solution)/shard_map/ppermute | solution.py:57
  124.8 90.5 %collective-permute-start.4 = (f32[1,4,64,1024]{3,2,1,0:T(8,128)S(1)}, f32[1,4,64,1024]{3,2,1,0:T(8,128)}, u32[]{:S(2)}, u32[]{:S(2)}) collective-permute-start(f32[1,4,64,1024]{3,2,1,0:T(8,128)S(1)} %get-tuple-element.43), channel_id=1, source_target_pairs={{0,5},{1,4},{2,7},{3,6},{4,1},{5,0},{6,3},{7,2},{8,13},{9,12},{10,... | collective-permute-start | bytes 3145736 | tf_op jit(solution)/shard_map/ppermute | solution.py:57
  125.1 92.5 %collective-permute-start.5 = (f32[1,4,64,1024]{3,2,1,0:T(8,128)S(1)}, f32[1,4,64,1024]{3,2,1,0:T(8,128)S(1)}, u32[]{:S(2)}, u32[]{:S(2)}) collective-permute-start(f32[1,4,64,1024]{3,2,1,0:T(8,128)S(1)} %get-tuple-element.42), channel_id=1, source_target_pairs={{0,6},{1,7},{2,4},{3,5},{4,2},{5,3},{6,0},{7,1},{8,14},{9,15},{10,... | collective-permute-start | bytes 3145736 | tf_op jit(solution)/shard_map/ppermute | solution.py:57
  147.8 71.0 %collective-permute-start.6 = (f32[1,4,64,1024]{3,2,1,0:T(8,128)S(1)}, f32[1,4,64,1024]{3,2,1,0:T(8,128)S(1)}, u32[]{:S(2)}, u32[]{:S(2)}) collective-permute-start(f32[1,4,64,1024]{3,2,1,0:T(8,128)S(1)} %get-tuple-element.41), channel_id=1, source_target_pairs={{0,7},{1,6},{2,5},{3,4},{4,3},{5,2},{6,1},{7,0},{8,15},{9,14},{10,... | collective-permute-start | bytes 3145736 | tf_op jit(solution)/shard_map/ppermute | solution.py:57
  235.8 7.8 %copy-start.3 = (s32[4]{0:T(128)S(1)}, s32[4]{0:T(128)}, u32[]{:S(2)}) copy-start(s32[4]{0:T(128)} %param.7) | copy-start | bytes 52
  238.7 31.7 %all-to-all-start = ((f32[4,1,65536]{2,1,0:T(1,128)}), f32[4,1,65536]{2,1,0:T(1,128)S(1)}, u32[]{:S(2)}, u32[]{:S(2)}) async-start(f32[4,1,65536]{2,1,0:T(1,128)} %reshape.1672), calls=%async_computation | async-start | bytes 2097152 | tf_op jit(solution)/shard_map/all_to_all | solution.py:72
